TPU v7x, 512 devices: a whole 4x4x16 slice. The times are simulated.
512 devices in a mesh: dp: 4 (over x), context: 16 (over z_lo, core), head: 8 (over y, z_hi).
Axes of the slice: x: 4, y: 4, z: 16 (z_hi: 2, z_lo: 8; z = z_hi * 8 + z_lo), core: 2. Of those that a mesh axis runs over, the one named last changes fastest.
Arguments:
- hidden: bfloat16 [4, 3072, 4096], P('dp', 'context'), may hold values from -6 to 6
- queries: bfloat16 [4, 3072, 4096], P('dp', 'context', 'head'), may hold values from -216 to 216
- grad_out: bfloat16 [4, 3072, 4096], P('dp', 'context', 'head'), may hold values from -6 to 6
- segment: int32 [4, 3072], P('dp', 'context'), may hold values from 0 to 3, never falling along the last dimension, each value on 1 to 1920 neighbouring positions
- key_proj: bfloat16 [4096, 1024], P(('dp', 'context'), 'head'), may hold values from -0.09375 to 0.09375
- value_proj: bfloat16 [4096, 1024], P(('dp', 'context'), 'head'), may hold values from -0.09375 to 0.09375
Outputs:
- grad_queries: bfloat16 [4, 3072, 4096], P('dp', 'context', 'head')
- grad_key_proj: float32 [4096, 1024], P(('dp', 'context'), 'head')
- grad_value_proj: float32 [4096, 1024], P(('dp', 'context'), 'head')
Inputs may be any that keep to these rules, and one draw needn't show every extreme that they name: segment ids never fall along a trace; each trace has 4 segments, one of exactly 1920 tokens.
All inputs are finite; a program needn't handle non-finite values.
Results may differ from a plain program's by a relative error of at most 0.04.
The roundings to bfloat16 on the way count: a program that leaves them out, or rounds other values in their place, can miss the bound.
Values may be sent and summed in bfloat16 or wider, within the bound.
A program may use at most 64 MiB of HBM per device.

v0:
```python
import jax
import jax.numpy as jnp
from jax import lax
from jax.sharding import PartitionSpec as P

HEADS = 32
KV_HEADS = 8
HEAD_DIM = 128
far_below = -1e30


def passed_along(block, axis, distance):
    devices = range(lax.axis_size(axis))
    route = [((i - distance) % len(devices), i) for i in devices]
    return lax.ppermute(block, axis, route)


def body(hidden, queries, grad_out, segment, key_proj, value_proj):
    tok_rows = hidden.shape[1]
    local_rows = hidden[0]
    kv_local = key_proj.shape[1] // HEAD_DIM
    group = HEADS // KV_HEADS
    scale = HEAD_DIM ** (-0.5)
    steps = lax.axis_size("context")
    pieces = (
        lax.all_gather(key_proj, ("dp", "context"), axis=0, tiled=True),
        lax.all_gather(value_proj, ("dp", "context"), axis=0, tiled=True),
    )
    columns = local_rows
    key_sum = jnp.dot(columns, pieces[0], preferred_element_type=jnp.float32)
    value_sum = jnp.dot(columns, pieces[1], preferred_element_type=jnp.float32)
    keys = key_sum.astype(jnp.bfloat16).reshape(tok_rows, kv_local, HEAD_DIM)
    values = value_sum.astype(jnp.bfloat16).reshape(tok_rows, kv_local, HEAD_DIM)
    marks = segment[0].astype(jnp.bfloat16)
    query_heads = queries[0].reshape(tok_rows, kv_local, group, HEAD_DIM)
    cot_heads = grad_out[0].reshape(tok_rows, kv_local, group, HEAD_DIM)

    def masked_scores(key_part, mark_part):
        raw = (
            jnp.einsum("qhgd,khd->qhgk", query_heads, key_part, preferred_element_type=jnp.float32)
            * scale
        )
        same = (marks[:, None] == mark_part[None, :])[:, None, None, :]
        return (jnp.where(same, raw, far_below), same)

    buffers = ()
    stat_shape = (tok_rows, kv_local, group)
    pieces = (
        lax.all_gather(keys, "context", axis=0, tiled=True),
        lax.all_gather(values, "context", axis=0, tiled=True),
        lax.all_gather(marks, "context", axis=0, tiled=True),
    )
    top = jnp.full(stat_shape, far_below, jnp.float32)
    stored = buffers
    raw, same = masked_scores(pieces[0], pieces[2])
    new_top = jnp.maximum(top, jnp.max(raw, axis=-1))
    weights = jnp.where(same, jnp.exp(raw - new_top[..., None]), 0.0)
    total = jnp.sum(weights, axis=-1)
    acc = jnp.einsum(
        "qhgk,khd->qhgd",
        weights.astype(jnp.bfloat16),
        pieces[1],
        preferred_element_type=jnp.float32,
    )
    top, total, acc, stored = (new_top, total, acc, stored)
    output = (acc / total[..., None]).astype(jnp.bfloat16)
    log_total = top + jnp.log(total)
    delta = jnp.sum(cot_heads.astype(jnp.float32) * output.astype(jnp.float32), axis=-1)

    def visit(key_part, value_part, mark_part, query_acc):
        raw, same = masked_scores(key_part, mark_part)
        probs = jnp.where(same, jnp.exp(raw - log_total[..., None]), 0.0)
        probs_b = probs.astype(jnp.bfloat16)
        value_part_grad = jnp.einsum(
            "qhgk,qhgd->khd", probs_b, cot_heads, preferred_element_type=jnp.float32
        )
        prob_grad = jnp.einsum(
            "qhgd,khd->qhgk", cot_heads, value_part, preferred_element_type=jnp.float32
        )
        dscores = (probs * (prob_grad - delta[..., None])).astype(jnp.bfloat16)
        query_acc = (
            query_acc
            + jnp.einsum("qhgk,khd->qhgd", dscores, key_part, preferred_element_type=jnp.float32)
            * scale
        )
        key_part_grad = (
            jnp.einsum("qhgk,qhgd->khd", dscores, query_heads, preferred_element_type=jnp.float32)
            * scale
        )
        return (query_acc, key_part_grad, value_part_grad)

    zero_grads = jnp.zeros((tok_rows, kv_local, HEAD_DIM), jnp.float32)
    query_zero = jnp.zeros((tok_rows, kv_local, group, HEAD_DIM), jnp.float32)

    def turn(index, state):
        key_part, value_part, mark_part, key_grad, value_grad, query_acc = state
        query_acc, key_more, value_more = visit(key_part, value_part, mark_part, query_acc)
        key_part, value_part, mark_part = passed_along(
            (key_part, value_part, mark_part), "context", 1
        )
        key_grad, value_grad = passed_along(
            (key_grad + key_more, value_grad + value_more), "context", 1
        )
        return (key_part, value_part, mark_part, key_grad, value_grad, query_acc)

    state = lax.fori_loop(0, steps, turn, (keys, values, marks, zero_grads, zero_grads, query_zero))
    key_grad, value_grad, query_acc = (state[3], state[4], state[5])
    grad_queries = query_acc.astype(jnp.bfloat16).reshape(1, tok_rows, kv_local * group * HEAD_DIM)
    both_grads = jnp.concatenate(
        [
            key_grad.astype(jnp.bfloat16).reshape(tok_rows, kv_local * HEAD_DIM),
            value_grad.astype(jnp.bfloat16).reshape(tok_rows, kv_local * HEAD_DIM),
        ],
        1,
    )
    columns = local_rows
    summed = lax.psum_scatter(
        jnp.einsum("td,tc->dc", columns, both_grads, preferred_element_type=jnp.float32),
        ("dp", "context"),
        scatter_dimension=0,
        tiled=True,
    )
    width_kv = key_proj.shape[1]
    return (grad_queries, summed[:, :width_kv], summed[:, width_kv:])


def solution(mesh):
    placed = (
        P("dp", "context", None),
        P("dp", "context", "head"),
        P("dp", "context", "head"),
        P("dp", "context"),
        P(("dp", "context"), "head"),
        P(("dp", "context"), "head"),
    )
    return jax.shard_map(
        body,
        mesh=mesh,
        in_specs=placed,
        out_specs=(
            P("dp", "context", "head"),
            P(("dp", "context"), "head"),
            P(("dp", "context"), "head"),
        ),
        check_vma=False,
    )
```

profile of v0, /device:TPU:8, one launch (start us, length us, event | category | flops | bytes accessed | tf_op | source)
XLA Modules:
  0.0 1097.5 jit_solution(6544349401803940098)
XLA Ops:
  13.6 56.4 %all-reduce = bf16[3072]{0:T(1024)(128)(2,1)S(1)} all-reduce(bf16[3072]{0:T(1024)(128)(2,1)S(1)} %dynamic-update-slice), channel_id=2, replica_groups=mesh['dp'=4,'context'=16,'head'=8] {'context'}, use_global_device_ids=true, to_apply=%add | all-reduce | flops 3072 | bytes 12288
  71.5 62.4 %all-gather.6.cloned.1.call-done = bf16[4096,128]{1,0:T(8,128)(2,1)} async-done(((bf16[64,128]{1,0:T(8,128)(2,1)}), bf16[4096,128]{1,0:T(8,128)(2,1)}) %all-gather.6.cloned.1.call-update) | async-done | bytes 1048592 | tf_op jit(solution)/shard_map/all_gather | solution.py:26
  135.6 33.5 %all-gather.1 = bf16[3072,128]{1,0:T(8,128)(2,1)S(1)} all-gather(bf16[192,128]{1,0:T(8,128)(2,1)S(1)} %fusion.40), channel_id=3, replica_groups=mesh['dp'=4,'context'=16,'head'=8] {'context'}, dimensions={0}, use_global_device_ids=true | all-gather | bytes 835584 | tf_op jit(solution)/shard_map/all_gather | solution.py:49
  169.1 5.6 fusion.25
  174.7 76.3 %all-gather.8.cloned.1.call-done = bf16[4096,128]{1,0:T(8,128)(2,1)} async-done(((bf16[64,128]{1,0:T(8,128)(2,1)}), bf16[4096,128]{1,0:T(8,128)(2,1)}) %all-gather.8.cloned.1.call-update) | async-done | bytes 1048592 | tf_op jit(solution)/shard_map/all_gather | solution.py:27
  252.9 33.5 %all-gather.2 = bf16[3072,128]{1,0:T(8,128)(2,1)S(1)} all-gather(bf16[192,128]{1,0:T(8,128)(2,1)S(1)} %fusion.43), channel_id=4, replica_groups=mesh['dp'=4,'context'=16,'head'=8] {'context'}, dimensions={0}, use_global_device_ids=true | all-gather | bytes 835584 | tf_op jit(solution)/shard_map/all_gather | solution.py:50
  286.4 6.5 fusion.27
  295.7 346.3 %while.21 = (s32[]{:T(128)}, bf16[192,1,128]{2,0,1:T(8,128)(2,1)S(1)}, bf16[192,1,128]{2,0,1:T(8,128)(2,1)S(1)}, bf16[192]{0:T(256)(128)(2,1)S(1)}, f32[192,1,12...) while((s32[]{:T(128)}, ...), condition=%wide.region_4.5_spmd.clone, body=%wide.region_3.4_spmd.clone.sunk | while | flops 190328832 | bytes 6227287 | solution.py:106
  311.4 4.1 collective-permute-done.3
  333.0 4.1 collective-permute-done.3
  350.7 3.9 collective-permute-done.2
  354.6 4.1 collective-permute-done.3
  376.2 4.1 collective-permute-done.3
  397.8 4.1 collective-permute-done.3
  415.5 3.9 collective-permute-done.2
  419.5 4.1 collective-permute-done.3
  437.2 3.9 collective-permute-done.2
  441.1 4.1 collective-permute-done.3
  458.8 3.9 collective-permute-done.2
  462.7 4.1 collective-permute-done.3
  484.3 4.1 collective-permute-done.3
  505.9 4.1 collective-permute-done.3
  527.6 4.1 collective-permute-done.3
  549.2 4.1 collective-permute-done.3
  566.9 3.9 collective-permute-done.2
  570.8 4.1 collective-permute-done.3
  592.4 4.1 collective-permute-done.3
  614.0 4.1 collective-permute-done.3
  631.7 3.9 collective-permute-done.2
  635.7 4.1 collective-permute-done.3
  644.7 5.6 copy.31
  651.2 438.3 %reduce-scatter.4.cloned.1.call-done = f32[64,256]{1,0:T(8,128)} async-done(((f32[4096,256]{1,0:T(8,128)}), f32[64,256]{1,0:T(8,128)}) %reduce-scatter.4.cloned.1.call-update) | async-done | bytes 65552
  (317 shorter events, 274.7 us)
Async XLA Ops:
  7.2 126.7 %all-gather.6.cloned.1.call-start = ((), (), s32[]{:S(2)}) async-start(), calls=%async_computation.1 | async-start | bytes 1064960 | tf_op jit(solution)/shard_map/all_gather | solution.py:26
  7.9 243.1 %all-gather.8.cloned.1.call-start = ((), (), s32[]{:S(2)}) async-start(), calls=%async_computation.2 | async-start | bytes 1064960 | tf_op jit(solution)/shard_map/all_gather | solution.py:27
  8.7 1080.9 %reduce-scatter.4.cloned.1.call-start = ((), (), s32[]{:S(2)}) async-start(), calls=%async_computation.3 | async-start | bytes 4259840
  295.7 15.7 %collective-permute-start = (bf16[192,1,128]{2,0,1:T(8,128)(2,1)S(1)}, bf16[192,1,128]{2,0,1:T(8,128)(2,1)S(1)}, u32[]{:S(2)}, u32[]{:S(2)}) collective-permute-start(bf16[192,1,128]{2,0,1:T(8,128)(2,1)S(1)} %copy.49), channel_id=1, source_target_pairs={{120,0},{0,8},{8,16},{16,24},{24,32},{32,40},{40,48},{48,56},{56,6... | collective-permute-start | bytes 147464 | tf_op jit(solution)/shard_map/while/body/eval_jaxpr/ppermute | solution.py:15
  298.0 13.4 %collective-permute-start.1 = (bf16[192,1,128]{2,0,1:T(8,128)(2,1)S(1)}, bf16[192,1,128]{2,0,1:T(8,128)(2,1)S(1)}, u32[]{:S(2)}, u32[]{:S(2)}) collective-permute-start(bf16[192,1,128]{2,0,1:T(8,128)(2,1)S(1)} %copy.50), channel_id=1, source_target_pairs={{120,0},{0,8},{8,16},{16,24},{24,32},{32,40},{40,48},{48,56},{56,6... | collective-permute-start | bytes 147464 | tf_op jit(solution)/shard_map/while/body/eval_jaxpr/ppermute | solution.py:15
  317.7 15.3 %collective-permute-start = (bf16[192,1,128]{2,0,1:T(8,128)(2,1)S(1)}, bf16[192,1,128]{2,0,1:T(8,128)(2,1)S(1)}, u32[]{:S(2)}, u32[]{:S(2)}) collective-permute-start(bf16[192,1,128]{2,0,1:T(8,128)(2,1)S(1)} %copy.49), channel_id=1, source_target_pairs={{120,0},{0,8},{8,16},{16,24},{24,32},{32,40},{40,48},{48,56},{56,6... | collective-permute-start | bytes 147464 | tf_op jit(solution)/shard_map/while/body/eval_jaxpr/ppermute | solution.py:15
  319.6 13.4 %collective-permute-start.1 = (bf16[192,1,128]{2,0,1:T(8,128)(2,1)S(1)}, bf16[192,1,128]{2,0,1:T(8,128)(2,1)S(1)}, u32[]{:S(2)}, u32[]{:S(2)}) collective-permute-start(bf16[192,1,128]{2,0,1:T(8,128)(2,1)S(1)} %copy.50), channel_id=1, source_target_pairs={{120,0},{0,8},{8,16},{16,24},{24,32},{32,40},{40,48},{48,56},{56,6... | collective-permute-start | bytes 147464 | tf_op jit(solution)/shard_map/while/body/eval_jaxpr/ppermute | solution.py:15
  339.3 15.3 %collective-permute-start = (bf16[192,1,128]{2,0,1:T(8,128)(2,1)S(1)}, bf16[192,1,128]{2,0,1:T(8,128)(2,1)S(1)}, u32[]{:S(2)}, u32[]{:S(2)}) collective-permute-start(bf16[192,1,128]{2,0,1:T(8,128)(2,1)S(1)} %copy.49), channel_id=1, source_target_pairs={{120,0},{0,8},{8,16},{16,24},{24,32},{32,40},{40,48},{48,56},{56,6... | collective-permute-start | bytes 147464 | tf_op jit(solution)/shard_map/while/body/eval_jaxpr/ppermute | solution.py:15
  341.2 13.4 %collective-permute-start.1 = (bf16[192,1,128]{2,0,1:T(8,128)(2,1)S(1)}, bf16[192,1,128]{2,0,1:T(8,128)(2,1)S(1)}, u32[]{:S(2)}, u32[]{:S(2)}) collective-permute-start(bf16[192,1,128]{2,0,1:T(8,128)(2,1)S(1)} %copy.50), channel_id=1, source_target_pairs={{120,0},{0,8},{8,16},{16,24},{24,32},{32,40},{40,48},{48,56},{56,6... | collective-permute-start | bytes 147464 | tf_op jit(solution)/shard_map/while/body/eval_jaxpr/ppermute | solution.py:15
  360.9 15.3 %collective-permute-start = (bf16[192,1,128]{2,0,1:T(8,128)(2,1)S(1)}, bf16[192,1,128]{2,0,1:T(8,128)(2,1)S(1)}, u32[]{:S(2)}, u32[]{:S(2)}) collective-permute-start(bf16[192,1,128]{2,0,1:T(8,128)(2,1)S(1)} %copy.49), channel_id=1, source_target_pairs={{120,0},{0,8},{8,16},{16,24},{24,32},{32,40},{40,48},{48,56},{56,6... | collective-permute-start | bytes 147464 | tf_op jit(solution)/shard_map/while/body/eval_jaxpr/ppermute | solution.py:15
  362.8 13.4 %collective-permute-start.1 = (bf16[192,1,128]{2,0,1:T(8,128)(2,1)S(1)}, bf16[192,1,128]{2,0,1:T(8,128)(2,1)S(1)}, u32[]{:S(2)}, u32[]{:S(2)}) collective-permute-start(bf16[192,1,128]{2,0,1:T(8,128)(2,1)S(1)} %copy.50), channel_id=1, source_target_pairs={{120,0},{0,8},{8,16},{16,24},{24,32},{32,40},{40,48},{48,56},{56,6... | collective-permute-start | bytes 147464 | tf_op jit(solution)/shard_map/while/body/eval_jaxpr/ppermute | solution.py:15
  382.5 15.3 %collective-permute-start = (bf16[192,1,128]{2,0,1:T(8,128)(2,1)S(1)}, bf16[192,1,128]{2,0,1:T(8,128)(2,1)S(1)}, u32[]{:S(2)}, u32[]{:S(2)}) collective-permute-start(bf16[192,1,128]{2,0,1:T(8,128)(2,1)S(1)} %copy.49), channel_id=1, source_target_pairs={{120,0},{0,8},{8,16},{16,24},{24,32},{32,40},{40,48},{48,56},{56,6... | collective-permute-start | bytes 147464 | tf_op jit(solution)/shard_map/while/body/eval_jaxpr/ppermute | solution.py:15
  384.4 13.4 %collective-permute-start.1 = (bf16[192,1,128]{2,0,1:T(8,128)(2,1)S(1)}, bf16[192,1,128]{2,0,1:T(8,128)(2,1)S(1)}, u32[]{:S(2)}, u32[]{:S(2)}) collective-permute-start(bf16[192,1,128]{2,0,1:T(8,128)(2,1)S(1)} %copy.50), channel_id=1, source_target_pairs={{120,0},{0,8},{8,16},{16,24},{24,32},{32,40},{40,48},{48,56},{56,6... | collective-permute-start | bytes 147464 | tf_op jit(solution)/shard_map/while/body/eval_jaxpr/ppermute | solution.py:15
  404.1 15.3 %collective-permute-start = (bf16[192,1,128]{2,0,1:T(8,128)(2,1)S(1)}, bf16[192,1,128]{2,0,1:T(8,128)(2,1)S(1)}, u32[]{:S(2)}, u32[]{:S(2)}) collective-permute-start(bf16[192,1,128]{2,0,1:T(8,128)(2,1)S(1)} %copy.49), channel_id=1, source_target_pairs={{120,0},{0,8},{8,16},{16,24},{24,32},{32,40},{40,48},{48,56},{56,6... | collective-permute-start | bytes 147464 | tf_op jit(solution)/shard_map/while/body/eval_jaxpr/ppermute | solution.py:15
  406.1 13.4 %collective-permute-start.1 = (bf16[192,1,128]{2,0,1:T(8,128)(2,1)S(1)}, bf16[192,1,128]{2,0,1:T(8,128)(2,1)S(1)}, u32[]{:S(2)}, u32[]{:S(2)}) collective-permute-start(bf16[192,1,128]{2,0,1:T(8,128)(2,1)S(1)} %copy.50), channel_id=1, source_target_pairs={{120,0},{0,8},{8,16},{16,24},{24,32},{32,40},{40,48},{48,56},{56,6... | collective-permute-start | bytes 147464 | tf_op jit(solution)/shard_map/while/body/eval_jaxpr/ppermute | solution.py:15
  425.7 15.3 %collective-permute-start = (bf16[192,1,128]{2,0,1:T(8,128)(2,1)S(1)}, bf16[192,1,128]{2,0,1:T(8,128)(2,1)S(1)}, u32[]{:S(2)}, u32[]{:S(2)}) collective-permute-start(bf16[192,1,128]{2,0,1:T(8,128)(2,1)S(1)} %copy.49), channel_id=1, source_target_pairs={{120,0},{0,8},{8,16},{16,24},{24,32},{32,40},{40,48},{48,56},{56,6... | collective-permute-start | bytes 147464 | tf_op jit(solution)/shard_map/while/body/eval_jaxpr/ppermute | solution.py:15
  427.7 13.4 %collective-permute-start.1 = (bf16[192,1,128]{2,0,1:T(8,128)(2,1)S(1)}, bf16[192,1,128]{2,0,1:T(8,128)(2,1)S(1)}, u32[]{:S(2)}, u32[]{:S(2)}) collective-permute-start(bf16[192,1,128]{2,0,1:T(8,128)(2,1)S(1)} %copy.50), channel_id=1, source_target_pairs={{120,0},{0,8},{8,16},{16,24},{24,32},{32,40},{40,48},{48,56},{56,6... | collective-permute-start | bytes 147464 | tf_op jit(solution)/shard_map/while/body/eval_jaxpr/ppermute | solution.py:15
  447.4 15.3 %collective-permute-start = (bf16[192,1,128]{2,0,1:T(8,128)(2,1)S(1)}, bf16[192,1,128]{2,0,1:T(8,128)(2,1)S(1)}, u32[]{:S(2)}, u32[]{:S(2)}) collective-permute-start(bf16[192,1,128]{2,0,1:T(8,128)(2,1)S(1)} %copy.49), channel_id=1, source_target_pairs={{120,0},{0,8},{8,16},{16,24},{24,32},{32,40},{40,48},{48,56},{56,6... | collective-permute-start | bytes 147464 | tf_op jit(solution)/shard_map/while/body/eval_jaxpr/ppermute | solution.py:15
  449.3 13.4 %collective-permute-start.1 = (bf16[192,1,128]{2,0,1:T(8,128)(2,1)S(1)}, bf16[192,1,128]{2,0,1:T(8,128)(2,1)S(1)}, u32[]{:S(2)}, u32[]{:S(2)}) collective-permute-start(bf16[192,1,128]{2,0,1:T(8,128)(2,1)S(1)} %copy.50), channel_id=1, source_target_pairs={{120,0},{0,8},{8,16},{16,24},{24,32},{32,40},{40,48},{48,56},{56,6... | collective-permute-start | bytes 147464 | tf_op jit(solution)/shard_map/while/body/eval_jaxpr/ppermute | solution.py:15
  469.0 15.3 %collective-permute-start = (bf16[192,1,128]{2,0,1:T(8,128)(2,1)S(1)}, bf16[192,1,128]{2,0,1:T(8,128)(2,1)S(1)}, u32[]{:S(2)}, u32[]{:S(2)}) collective-permute-start(bf16[192,1,128]{2,0,1:T(8,128)(2,1)S(1)} %copy.49), channel_id=1, source_target_pairs={{120,0},{0,8},{8,16},{16,24},{24,32},{32,40},{40,48},{48,56},{56,6... | collective-permute-start | bytes 147464 | tf_op jit(solution)/shard_map/while/body/eval_jaxpr/ppermute | solution.py:15
  470.9 13.4 %collective-permute-start.1 = (bf16[192,1,128]{2,0,1:T(8,128)(2,1)S(1)}, bf16[192,1,128]{2,0,1:T(8,128)(2,1)S(1)}, u32[]{:S(2)}, u32[]{:S(2)}) collective-permute-start(bf16[192,1,128]{2,0,1:T(8,128)(2,1)S(1)} %copy.50), channel_id=1, source_target_pairs={{120,0},{0,8},{8,16},{16,24},{24,32},{32,40},{40,48},{48,56},{56,6... | collective-permute-start | bytes 147464 | tf_op jit(solution)/shard_map/while/body/eval_jaxpr/ppermute | solution.py:15
  490.6 15.3 %collective-permute-start = (bf16[192,1,128]{2,0,1:T(8,128)(2,1)S(1)}, bf16[192,1,128]{2,0,1:T(8,128)(2,1)S(1)}, u32[]{:S(2)}, u32[]{:S(2)}) collective-permute-start(bf16[192,1,128]{2,0,1:T(8,128)(2,1)S(1)} %copy.49), channel_id=1, source_target_pairs={{120,0},{0,8},{8,16},{16,24},{24,32},{32,40},{40,48},{48,56},{56,6... | collective-permute-start | bytes 147464 | tf_op jit(solution)/shard_map/while/body/eval_jaxpr/ppermute | solution.py:15
  492.5 13.4 %collective-permute-start.1 = (bf16[192,1,128]{2,0,1:T(8,128)(2,1)S(1)}, bf16[192,1,128]{2,0,1:T(8,128)(2,1)S(1)}, u32[]{:S(2)}, u32[]{:S(2)}) collective-permute-start(bf16[192,1,128]{2,0,1:T(8,128)(2,1)S(1)} %copy.50), channel_id=1, source_target_pairs={{120,0},{0,8},{8,16},{16,24},{24,32},{32,40},{40,48},{48,56},{56,6... | collective-permute-start | bytes 147464 | tf_op jit(solution)/shard_map/while/body/eval_jaxpr/ppermute | solution.py:15
  512.2 15.3 %collective-permute-start = (bf16[192,1,128]{2,0,1:T(8,128)(2,1)S(1)}, bf16[192,1,128]{2,0,1:T(8,128)(2,1)S(1)}, u32[]{:S(2)}, u32[]{:S(2)}) collective-permute-start(bf16[192,1,128]{2,0,1:T(8,128)(2,1)S(1)} %copy.49), channel_id=1, source_target_pairs={{120,0},{0,8},{8,16},{16,24},{24,32},{32,40},{40,48},{48,56},{56,6... | collective-permute-start | bytes 147464 | tf_op jit(solution)/shard_map/while/body/eval_jaxpr/ppermute | solution.py:15
  514.2 13.4 %collective-permute-start.1 = (bf16[192,1,128]{2,0,1:T(8,128)(2,1)S(1)}, bf16[192,1,128]{2,0,1:T(8,128)(2,1)S(1)}, u32[]{:S(2)}, u32[]{:S(2)}) collective-permute-start(bf16[192,1,128]{2,0,1:T(8,128)(2,1)S(1)} %copy.50), channel_id=1, source_target_pairs={{120,0},{0,8},{8,16},{16,24},{24,32},{32,40},{40,48},{48,56},{56,6... | collective-permute-start | bytes 147464 | tf_op jit(solution)/shard_map/while/body/eval_jaxpr/ppermute | solution.py:15
  533.8 15.3 %collective-permute-start = (bf16[192,1,128]{2,0,1:T(8,128)(2,1)S(1)}, bf16[192,1,128]{2,0,1:T(8,128)(2,1)S(1)}, u32[]{:S(2)}, u32[]{:S(2)}) collective-permute-start(bf16[192,1,128]{2,0,1:T(8,128)(2,1)S(1)} %copy.49), channel_id=1, source_target_pairs={{120,0},{0,8},{8,16},{16,24},{24,32},{32,40},{40,48},{48,56},{56,6... | collective-permute-start | bytes 147464 | tf_op jit(solution)/shard_map/while/body/eval_jaxpr/ppermute | solution.py:15
  535.8 13.4 %collective-permute-start.1 = (bf16[192,1,128]{2,0,1:T(8,128)(2,1)S(1)}, bf16[192,1,128]{2,0,1:T(8,128)(2,1)S(1)}, u32[]{:S(2)}, u32[]{:S(2)}) collective-permute-start(bf16[192,1,128]{2,0,1:T(8,128)(2,1)S(1)} %copy.50), channel_id=1, source_target_pairs={{120,0},{0,8},{8,16},{16,24},{24,32},{32,40},{40,48},{48,56},{56,6... | collective-permute-start | bytes 147464 | tf_op jit(solution)/shard_map/while/body/eval_jaxpr/ppermute | solution.py:15
  555.5 15.3 %collective-permute-start = (bf16[192,1,128]{2,0,1:T(8,128)(2,1)S(1)}, bf16[192,1,128]{2,0,1:T(8,128)(2,1)S(1)}, u32[]{:S(2)}, u32[]{:S(2)}) collective-permute-start(bf16[192,1,128]{2,0,1:T(8,128)(2,1)S(1)} %copy.49), channel_id=1, source_target_pairs={{120,0},{0,8},{8,16},{16,24},{24,32},{32,40},{40,48},{48,56},{56,6... | collective-permute-start | bytes 147464 | tf_op jit(solution)/shard_map/while/body/eval_jaxpr/ppermute | solution.py:15
  557.4 13.4 %collective-permute-start.1 = (bf16[192,1,128]{2,0,1:T(8,128)(2,1)S(1)}, bf16[192,1,128]{2,0,1:T(8,128)(2,1)S(1)}, u32[]{:S(2)}, u32[]{:S(2)}) collective-permute-start(bf16[192,1,128]{2,0,1:T(8,128)(2,1)S(1)} %copy.50), channel_id=1, source_target_pairs={{120,0},{0,8},{8,16},{16,24},{24,32},{32,40},{40,48},{48,56},{56,6... | collective-permute-start | bytes 147464 | tf_op jit(solution)/shard_map/while/body/eval_jaxpr/ppermute | solution.py:15
  577.1 15.3 %collective-permute-start = (bf16[192,1,128]{2,0,1:T(8,128)(2,1)S(1)}, bf16[192,1,128]{2,0,1:T(8,128)(2,1)S(1)}, u32[]{:S(2)}, u32[]{:S(2)}) collective-permute-start(bf16[192,1,128]{2,0,1:T(8,128)(2,1)S(1)} %copy.49), channel_id=1, source_target_pairs={{120,0},{0,8},{8,16},{16,24},{24,32},{32,40},{40,48},{48,56},{56,6... | collective-permute-start | bytes 147464 | tf_op jit(solution)/shard_map/while/body/eval_jaxpr/ppermute | solution.py:15
  598.7 15.3 %collective-permute-start = (bf16[192,1,128]{2,0,1:T(8,128)(2,1)S(1)}, bf16[192,1,128]{2,0,1:T(8,128)(2,1)S(1)}, u32[]{:S(2)}, u32[]{:S(2)}) collective-permute-start(bf16[192,1,128]{2,0,1:T(8,128)(2,1)S(1)} %copy.49), channel_id=1, source_target_pairs={{120,0},{0,8},{8,16},{16,24},{24,32},{32,40},{40,48},{48,56},{56,6... | collective-permute-start | bytes 147464 | tf_op jit(solution)/shard_map/while/body/eval_jaxpr/ppermute | solution.py:15
  620.3 15.3 %collective-permute-start = (bf16[192,1,128]{2,0,1:T(8,128)(2,1)S(1)}, bf16[192,1,128]{2,0,1:T(8,128)(2,1)S(1)}, u32[]{:S(2)}, u32[]{:S(2)}) collective-permute-start(bf16[192,1,128]{2,0,1:T(8,128)(2,1)S(1)} %copy.49), channel_id=1, source_target_pairs={{120,0},{0,8},{8,16},{16,24},{24,32},{32,40},{40,48},{48,56},{56,6... | collective-permute-start | bytes 147464 | tf_op jit(solution)/shard_map/while/body/eval_jaxpr/ppermute | solution.py:15
  (53 other events, 793.6 us)
Sparse Core Ops, SparseCore 0:
  10.2 123.6 all-gather.5
  136.0 114.9 all-gather.7
  650.4 439.0 reduce-scatter.3
where the time goes:
time: 1100 us
  waiting for transfers between devices  742 us (67%)
  starting transfers between devices  154 us (14%)
  blocking collectives  123 us (11%)
  matrix products  40.3 us (4%)
  between operations  14.5 us (1%)
  local copies, waits for them, and re-layouts  12.7 us (1%)
    unnamed x4, waiting for transfers between devices  440 us
    ppermute x80, waiting for transfers between devices, passed_along(): return lax.ppermute(block, axis, route)  163 us
    ppermute x80, starting transfers between devices, passed_along(): return lax.ppermute(block, axis, route)  154 us
    all_gather x1, waiting for transfers between devices, body(): lax.all_gather(value_proj, ('dp', 'context'), axis=0, tiled=True)  76.3 us
    all_gather x1, waiting for transfers between devices, body(): lax.all_gather(key_proj, ('dp', 'context'), axis=0, tiled=True)  62.4 us
    unnamed x1, blocking collectives  56.4 us
    all_gather x1, blocking collectives, body(): lax.all_gather(values, 'context', axis=0, tiled=True)  33.5 us
    all_gather x1, blocking collectives, body(): lax.all_gather(keys, 'context', axis=0, tiled=True)  33.5 us
  transfers between devices with their start and end apart: 83, of which 51 were waited for; matrix products, arithmetic and copies ran while one was open for 4% of the time, Pallas kernels for 0%

commit v1 on v0

--- a/solution.py
+++ b/solution.py
@@ -24,7 +24,12 @@
     steps = lax.axis_size("context")
     pieces = (
         lax.all_gather(key_proj, ("dp", "context"), axis=0, tiled=True),
-        lax.all_gather(value_proj, ("dp", "context"), axis=0, tiled=True),
+        jnp.concatenate(
+            lax.all_to_all(
+                jnp.stack([value_proj] * lax.axis_size(("dp", "context"))), ("dp", "context"), 0, 0
+            ),
+            axis=0,
+        ),
     )
     columns = local_rows
     key_sum = jnp.dot(columns, pieces[0], preferred_element_type=jnp.float32)

time: 1100 us -> 1030 us (0.936)
  the two profiles are of different devices: /device:TPU:8 before, /device:TPU:16 now
where the time goes in v1:
time: 1030 us; the launch traced here: 1020 us
  waiting for transfers between devices  650 us (63%)
  starting transfers between devices  171 us (17%)
  blocking collectives  122 us (12%)
  matrix products  40.2 us (4%)
  local copies, waits for them, and re-layouts  18.2 us (2%)
  between operations  14.9 us (1%)
    unnamed x3, waiting for transfers between devices  439 us
    ppermute x80, waiting for transfers between devices, passed_along(): return lax.ppermute(block, axis, route)  163 us
    ppermute x80, starting transfers between devices, passed_along(): return lax.ppermute(block, axis, route)  155 us
    unnamed x1, blocking collectives  58.9 us
    all_gather x1, waiting for transfers between devices, body(): lax.all_gather(key_proj, ('dp', 'context'), axis=0, tiled=True)  47.9 us
    all_gather x1, blocking collectives, body(): lax.all_gather(keys, 'context', axis=0, tiled=True)  33.9 us
    all_gather x1, blocking collectives, body(): lax.all_gather(values, 'context', axis=0, tiled=True)  29.6 us
  transfers between devices with their start and end apart: 83, of which 50 were waited for; matrix products, arithmetic and copies ran while one was open for 4% of the time, Pallas kernels for 0%

profile of v1, /device:TPU:16, one launch (start us, length us, event | category | flops | bytes accessed | tf_op | source)
XLA Modules:
  0.0 1024.5 jit_solution(718537736535189762)
XLA Ops:
  9.9 16.3 %all-to-all-start = ((bf16[64,64,128]{2,1,0:T(8,128)(2,1)}), bf16[64,64,128]{2,1,0:T(8,128)(2,1)}, u32[]{:S(2)}, u32[]{:S(2)}) async-start(bf16[64,64,128]{2,1,0:T(8,128)(2,1)} %stack.2), calls=%async_computation | async-start | bytes 2097152 | tf_op jit(solution)/shard_map/all_to_all | solution.py:28
  32.1 58.9 %all-reduce = bf16[3072]{0:T(1024)(128)(2,1)S(1)} all-reduce(bf16[3072]{0:T(1024)(128)(2,1)S(1)} %dynamic-update-slice), channel_id=2, replica_groups=mesh['dp'=4,'context'=16,'head'=8] {'context'}, use_global_device_ids=true, to_apply=%add | all-reduce | flops 3072 | bytes 12288
  91.4 47.9 %all-gather.5.cloned.1.call-done = bf16[4096,128]{1,0:T(8,128)(2,1)} async-done(((bf16[64,128]{1,0:T(8,128)(2,1)}), bf16[4096,128]{1,0:T(8,128)(2,1)}) %all-gather.5.cloned.1.call-update) | async-done | bytes 1048592 | tf_op jit(solution)/shard_map/all_gather | solution.py:26
  141.1 33.9 %all-gather.1 = bf16[3072,128]{1,0:T(8,128)(2,1)S(1)} all-gather(bf16[192,128]{1,0:T(8,128)(2,1)S(1)} %fusion.40), channel_id=3, replica_groups=mesh['dp'=4,'context'=16,'head'=8] {'context'}, dimensions={0}, use_global_device_ids=true | all-gather | bytes 835584 | tf_op jit(solution)/shard_map/all_gather | solution.py:54
  185.7 29.6 %all-gather.2 = bf16[3072,128]{1,0:T(8,128)(2,1)S(1)} all-gather(bf16[192,128]{1,0:T(8,128)(2,1)S(1)} %fusion.43), channel_id=4, replica_groups=mesh['dp'=4,'context'=16,'head'=8] {'context'}, dimensions={0}, use_global_device_ids=true | all-gather | bytes 835584 | tf_op jit(solution)/shard_map/all_gather | solution.py:55
  215.2 6.2 fusion.61
  221.5 347.1 %while.21 = (s32[]{:T(128)}, bf16[192,1,128]{2,0,1:T(8,128)(2,1)S(1)}, bf16[192,1,128]{2,0,1:T(8,128)(2,1)S(1)}, bf16[192]{0:T(256)(128)(2,1)S(1)}, f32[192,1,12...) while((s32[]{:T(128)}, ...), condition=%wide.region_4.5_spmd.clone, body=%wide.region_3.4_spmd.clone.sunk | while | flops 190328832 | bytes 6227287 | solution.py:111
  237.7 4.4 collective-permute-done.3
  259.6 4.1 collective-permute-done.3
  277.3 3.9 collective-permute-done.2
  281.2 4.1 collective-permute-done.3
  298.9 3.9 collective-permute-done.2
  302.8 4.1 collective-permute-done.3
  324.5 4.1 collective-permute-done.3
  342.2 3.9 collective-permute-done.2
  346.1 4.1 collective-permute-done.3
  363.8 3.9 collective-permute-done.2
  367.7 4.1 collective-permute-done.3
  389.3 4.1 collective-permute-done.3
  407.0 3.9 collective-permute-done.2
  410.9 4.1 collective-permute-done.3
  432.6 4.1 collective-permute-done.3
  454.2 4.1 collective-permute-done.3
  471.9 3.9 collective-permute-done.2
  475.8 4.1 collective-permute-done.3
  497.4 4.1 collective-permute-done.3
  519.0 4.1 collective-permute-done.3
  536.7 3.9 collective-permute-done.2
  540.7 4.1 collective-permute-done.3
  562.3 4.1 collective-permute-done.3
  571.3 5.6 copy.31
  577.9 438.5 %reduce-scatter.4.cloned.1.call-done = f32[64,256]{1,0:T(8,128)} async-done(((f32[4096,256]{1,0:T(8,128)}), f32[64,256]{1,0:T(8,128)}) %reduce-scatter.4.cloned.1.call-update) | async-done | bytes 65552
  (317 shorter events, 278.5 us)
Async XLA Ops:
  7.2 132.1 %all-gather.5.cloned.1.call-start = ((), (), s32[]{:S(2)}) async-start(), calls=%async_computation.2 | async-start | bytes 1064960 | tf_op jit(solution)/shard_map/all_gather | solution.py:26
  9.9 174.0 %all-to-all-start = ((bf16[64,64,128]{2,1,0:T(8,128)(2,1)}), bf16[64,64,128]{2,1,0:T(8,128)(2,1)}, u32[]{:S(2)}, u32[]{:S(2)}) async-start(bf16[64,64,128]{2,1,0:T(8,128)(2,1)} %stack.2), calls=%async_computation | async-start | bytes 2097152 | tf_op jit(solution)/shard_map/all_to_all | solution.py:28
  26.1 990.2 %reduce-scatter.4.cloned.1.call-start = ((), (), s32[]{:S(2)}) async-start(), calls=%async_computation.3 | async-start | bytes 4259840
  221.5 16.2 %collective-permute-start = (bf16[192,1,128]{2,0,1:T(8,128)(2,1)S(1)}, bf16[192,1,128]{2,0,1:T(8,128)(2,1)S(1)}, u32[]{:S(2)}, u32[]{:S(2)}) collective-permute-start(bf16[192,1,128]{2,0,1:T(8,128)(2,1)S(1)} %copy.49), channel_id=1, source_target_pairs={{120,0},{0,8},{8,16},{16,24},{24,32},{32,40},{40,48},{48,56},{56,6... | collective-permute-start | bytes 147464 | tf_op jit(solution)/shard_map/while/body/eval_jaxpr/ppermute | solution.py:15
  223.8 13.9 %collective-permute-start.1 = (bf16[192,1,128]{2,0,1:T(8,128)(2,1)S(1)}, bf16[192,1,128]{2,0,1:T(8,128)(2,1)S(1)}, u32[]{:S(2)}, u32[]{:S(2)}) collective-permute-start(bf16[192,1,128]{2,0,1:T(8,128)(2,1)S(1)} %copy.50), channel_id=1, source_target_pairs={{120,0},{0,8},{8,16},{16,24},{24,32},{32,40},{40,48},{48,56},{56,6... | collective-permute-start | bytes 147464 | tf_op jit(solution)/shard_map/while/body/eval_jaxpr/ppermute | solution.py:15
  244.3 15.3 %collective-permute-start = (bf16[192,1,128]{2,0,1:T(8,128)(2,1)S(1)}, bf16[192,1,128]{2,0,1:T(8,128)(2,1)S(1)}, u32[]{:S(2)}, u32[]{:S(2)}) collective-permute-start(bf16[192,1,128]{2,0,1:T(8,128)(2,1)S(1)} %copy.49), channel_id=1, source_target_pairs={{120,0},{0,8},{8,16},{16,24},{24,32},{32,40},{40,48},{48,56},{56,6... | collective-permute-start | bytes 147464 | tf_op jit(solution)/shard_map/while/body/eval_jaxpr/ppermute | solution.py:15
  246.2 13.4 %collective-permute-start.1 = (bf16[192,1,128]{2,0,1:T(8,128)(2,1)S(1)}, bf16[192,1,128]{2,0,1:T(8,128)(2,1)S(1)}, u32[]{:S(2)}, u32[]{:S(2)}) collective-permute-start(bf16[192,1,128]{2,0,1:T(8,128)(2,1)S(1)} %copy.50), channel_id=1, source_target_pairs={{120,0},{0,8},{8,16},{16,24},{24,32},{32,40},{40,48},{48,56},{56,6... | collective-permute-start | bytes 147464 | tf_op jit(solution)/shard_map/while/body/eval_jaxpr/ppermute | solution.py:15
  265.9 15.3 %collective-permute-start = (bf16[192,1,128]{2,0,1:T(8,128)(2,1)S(1)}, bf16[192,1,128]{2,0,1:T(8,128)(2,1)S(1)}, u32[]{:S(2)}, u32[]{:S(2)}) collective-permute-start(bf16[192,1,128]{2,0,1:T(8,128)(2,1)S(1)} %copy.49), channel_id=1, source_target_pairs={{120,0},{0,8},{8,16},{16,24},{24,32},{32,40},{40,48},{48,56},{56,6... | collective-permute-start | bytes 147464 | tf_op jit(solution)/shard_map/while/body/eval_jaxpr/ppermute | solution.py:15
  267.8 13.4 %collective-permute-start.1 = (bf16[192,1,128]{2,0,1:T(8,128)(2,1)S(1)}, bf16[192,1,128]{2,0,1:T(8,128)(2,1)S(1)}, u32[]{:S(2)}, u32[]{:S(2)}) collective-permute-start(bf16[192,1,128]{2,0,1:T(8,128)(2,1)S(1)} %copy.50), channel_id=1, source_target_pairs={{120,0},{0,8},{8,16},{16,24},{24,32},{32,40},{40,48},{48,56},{56,6... | collective-permute-start | bytes 147464 | tf_op jit(solution)/shard_map/while/body/eval_jaxpr/ppermute | solution.py:15
  287.5 15.3 %collective-permute-start = (bf16[192,1,128]{2,0,1:T(8,128)(2,1)S(1)}, bf16[192,1,128]{2,0,1:T(8,128)(2,1)S(1)}, u32[]{:S(2)}, u32[]{:S(2)}) collective-permute-start(bf16[192,1,128]{2,0,1:T(8,128)(2,1)S(1)} %copy.49), channel_id=1, source_target_pairs={{120,0},{0,8},{8,16},{16,24},{24,32},{32,40},{40,48},{48,56},{56,6... | collective-permute-start | bytes 147464 | tf_op jit(solution)/shard_map/while/body/eval_jaxpr/ppermute | solution.py:15
  289.4 13.4 %collective-permute-start.1 = (bf16[192,1,128]{2,0,1:T(8,128)(2,1)S(1)}, bf16[192,1,128]{2,0,1:T(8,128)(2,1)S(1)}, u32[]{:S(2)}, u32[]{:S(2)}) collective-permute-start(bf16[192,1,128]{2,0,1:T(8,128)(2,1)S(1)} %copy.50), channel_id=1, source_target_pairs={{120,0},{0,8},{8,16},{16,24},{24,32},{32,40},{40,48},{48,56},{56,6... | collective-permute-start | bytes 147464 | tf_op jit(solution)/shard_map/while/body/eval_jaxpr/ppermute | solution.py:15
  309.1 15.3 %collective-permute-start = (bf16[192,1,128]{2,0,1:T(8,128)(2,1)S(1)}, bf16[192,1,128]{2,0,1:T(8,128)(2,1)S(1)}, u32[]{:S(2)}, u32[]{:S(2)}) collective-permute-start(bf16[192,1,128]{2,0,1:T(8,128)(2,1)S(1)} %copy.49), channel_id=1, source_target_pairs={{120,0},{0,8},{8,16},{16,24},{24,32},{32,40},{40,48},{48,56},{56,6... | collective-permute-start | bytes 147464 | tf_op jit(solution)/shard_map/while/body/eval_jaxpr/ppermute | solution.py:15
  311.1 13.4 %collective-permute-start.1 = (bf16[192,1,128]{2,0,1:T(8,128)(2,1)S(1)}, bf16[192,1,128]{2,0,1:T(8,128)(2,1)S(1)}, u32[]{:S(2)}, u32[]{:S(2)}) collective-permute-start(bf16[192,1,128]{2,0,1:T(8,128)(2,1)S(1)} %copy.50), channel_id=1, source_target_pairs={{120,0},{0,8},{8,16},{16,24},{24,32},{32,40},{40,48},{48,56},{56,6... | collective-permute-start | bytes 147464 | tf_op jit(solution)/shard_map/while/body/eval_jaxpr/ppermute | solution.py:15
  330.7 15.3 %collective-permute-start = (bf16[192,1,128]{2,0,1:T(8,128)(2,1)S(1)}, bf16[192,1,128]{2,0,1:T(8,128)(2,1)S(1)}, u32[]{:S(2)}, u32[]{:S(2)}) collective-permute-start(bf16[192,1,128]{2,0,1:T(8,128)(2,1)S(1)} %copy.49), channel_id=1, source_target_pairs={{120,0},{0,8},{8,16},{16,24},{24,32},{32,40},{40,48},{48,56},{56,6... | collective-permute-start | bytes 147464 | tf_op jit(solution)/shard_map/while/body/eval_jaxpr/ppermute | solution.py:15
  332.7 13.4 %collective-permute-start.1 = (bf16[192,1,128]{2,0,1:T(8,128)(2,1)S(1)}, bf16[192,1,128]{2,0,1:T(8,128)(2,1)S(1)}, u32[]{:S(2)}, u32[]{:S(2)}) collective-permute-start(bf16[192,1,128]{2,0,1:T(8,128)(2,1)S(1)} %copy.50), channel_id=1, source_target_pairs={{120,0},{0,8},{8,16},{16,24},{24,32},{32,40},{40,48},{48,56},{56,6... | collective-permute-start | bytes 147464 | tf_op jit(solution)/shard_map/while/body/eval_jaxpr/ppermute | solution.py:15
  352.4 15.3 %collective-permute-start = (bf16[192,1,128]{2,0,1:T(8,128)(2,1)S(1)}, bf16[192,1,128]{2,0,1:T(8,128)(2,1)S(1)}, u32[]{:S(2)}, u32[]{:S(2)}) collective-permute-start(bf16[192,1,128]{2,0,1:T(8,128)(2,1)S(1)} %copy.49), channel_id=1, source_target_pairs={{120,0},{0,8},{8,16},{16,24},{24,32},{32,40},{40,48},{48,56},{56,6... | collective-permute-start | bytes 147464 | tf_op jit(solution)/shard_map/while/body/eval_jaxpr/ppermute | solution.py:15
  354.3 13.4 %collective-permute-start.1 = (bf16[192,1,128]{2,0,1:T(8,128)(2,1)S(1)}, bf16[192,1,128]{2,0,1:T(8,128)(2,1)S(1)}, u32[]{:S(2)}, u32[]{:S(2)}) collective-permute-start(bf16[192,1,128]{2,0,1:T(8,128)(2,1)S(1)} %copy.50), channel_id=1, source_target_pairs={{120,0},{0,8},{8,16},{16,24},{24,32},{32,40},{40,48},{48,56},{56,6... | collective-permute-start | bytes 147464 | tf_op jit(solution)/shard_map/while/body/eval_jaxpr/ppermute | solution.py:15
  374.0 15.3 %collective-permute-start = (bf16[192,1,128]{2,0,1:T(8,128)(2,1)S(1)}, bf16[192,1,128]{2,0,1:T(8,128)(2,1)S(1)}, u32[]{:S(2)}, u32[]{:S(2)}) collective-permute-start(bf16[192,1,128]{2,0,1:T(8,128)(2,1)S(1)} %copy.49), channel_id=1, source_target_pairs={{120,0},{0,8},{8,16},{16,24},{24,32},{32,40},{40,48},{48,56},{56,6... | collective-permute-start | bytes 147464 | tf_op jit(solution)/shard_map/while/body/eval_jaxpr/ppermute | solution.py:15
  375.9 13.4 %collective-permute-start.1 = (bf16[192,1,128]{2,0,1:T(8,128)(2,1)S(1)}, bf16[192,1,128]{2,0,1:T(8,128)(2,1)S(1)}, u32[]{:S(2)}, u32[]{:S(2)}) collective-permute-start(bf16[192,1,128]{2,0,1:T(8,128)(2,1)S(1)} %copy.50), channel_id=1, source_target_pairs={{120,0},{0,8},{8,16},{16,24},{24,32},{32,40},{40,48},{48,56},{56,6... | collective-permute-start | bytes 147464 | tf_op jit(solution)/shard_map/while/body/eval_jaxpr/ppermute | solution.py:15
  395.6 15.3 %collective-permute-start = (bf16[192,1,128]{2,0,1:T(8,128)(2,1)S(1)}, bf16[192,1,128]{2,0,1:T(8,128)(2,1)S(1)}, u32[]{:S(2)}, u32[]{:S(2)}) collective-permute-start(bf16[192,1,128]{2,0,1:T(8,128)(2,1)S(1)} %copy.49), channel_id=1, source_target_pairs={{120,0},{0,8},{8,16},{16,24},{24,32},{32,40},{40,48},{48,56},{56,6... | collective-permute-start | bytes 147464 | tf_op jit(solution)/shard_map/while/body/eval_jaxpr/ppermute | solution.py:15
  397.5 13.4 %collective-permute-start.1 = (bf16[192,1,128]{2,0,1:T(8,128)(2,1)S(1)}, bf16[192,1,128]{2,0,1:T(8,128)(2,1)S(1)}, u32[]{:S(2)}, u32[]{:S(2)}) collective-permute-start(bf16[192,1,128]{2,0,1:T(8,128)(2,1)S(1)} %copy.50), channel_id=1, source_target_pairs={{120,0},{0,8},{8,16},{16,24},{24,32},{32,40},{40,48},{48,56},{56,6... | collective-permute-start | bytes 147464 | tf_op jit(solution)/shard_map/while/body/eval_jaxpr/ppermute | solution.py:15
  417.2 15.3 %collective-permute-start = (bf16[192,1,128]{2,0,1:T(8,128)(2,1)S(1)}, bf16[192,1,128]{2,0,1:T(8,128)(2,1)S(1)}, u32[]{:S(2)}, u32[]{:S(2)}) collective-permute-start(bf16[192,1,128]{2,0,1:T(8,128)(2,1)S(1)} %copy.49), channel_id=1, source_target_pairs={{120,0},{0,8},{8,16},{16,24},{24,32},{32,40},{40,48},{48,56},{56,6... | collective-permute-start | bytes 147464 | tf_op jit(solution)/shard_map/while/body/eval_jaxpr/ppermute | solution.py:15
  419.2 13.4 %collective-permute-start.1 = (bf16[192,1,128]{2,0,1:T(8,128)(2,1)S(1)}, bf16[192,1,128]{2,0,1:T(8,128)(2,1)S(1)}, u32[]{:S(2)}, u32[]{:S(2)}) collective-permute-start(bf16[192,1,128]{2,0,1:T(8,128)(2,1)S(1)} %copy.50), channel_id=1, source_target_pairs={{120,0},{0,8},{8,16},{16,24},{24,32},{32,40},{40,48},{48,56},{56,6... | collective-permute-start | bytes 147464 | tf_op jit(solution)/shard_map/while/body/eval_jaxpr/ppermute | solution.py:15
  438.8 15.3 %collective-permute-start = (bf16[192,1,128]{2,0,1:T(8,128)(2,1)S(1)}, bf16[192,1,128]{2,0,1:T(8,128)(2,1)S(1)}, u32[]{:S(2)}, u32[]{:S(2)}) collective-permute-start(bf16[192,1,128]{2,0,1:T(8,128)(2,1)S(1)} %copy.49), channel_id=1, source_target_pairs={{120,0},{0,8},{8,16},{16,24},{24,32},{32,40},{40,48},{48,56},{56,6... | collective-permute-start | bytes 147464 | tf_op jit(solution)/shard_map/while/body/eval_jaxpr/ppermute | solution.py:15
  460.5 15.3 %collective-permute-start = (bf16[192,1,128]{2,0,1:T(8,128)(2,1)S(1)}, bf16[192,1,128]{2,0,1:T(8,128)(2,1)S(1)}, u32[]{:S(2)}, u32[]{:S(2)}) collective-permute-start(bf16[192,1,128]{2,0,1:T(8,128)(2,1)S(1)} %copy.49), channel_id=1, source_target_pairs={{120,0},{0,8},{8,16},{16,24},{24,32},{32,40},{40,48},{48,56},{56,6... | collective-permute-start | bytes 147464 | tf_op jit(solution)/shard_map/while/body/eval_jaxpr/ppermute | solution.py:15
  462.4 13.4 %collective-permute-start.1 = (bf16[192,1,128]{2,0,1:T(8,128)(2,1)S(1)}, bf16[192,1,128]{2,0,1:T(8,128)(2,1)S(1)}, u32[]{:S(2)}, u32[]{:S(2)}) collective-permute-start(bf16[192,1,128]{2,0,1:T(8,128)(2,1)S(1)} %copy.50), channel_id=1, source_target_pairs={{120,0},{0,8},{8,16},{16,24},{24,32},{32,40},{40,48},{48,56},{56,6... | collective-permute-start | bytes 147464 | tf_op jit(solution)/shard_map/while/body/eval_jaxpr/ppermute | solution.py:15
  482.1 15.3 %collective-permute-start = (bf16[192,1,128]{2,0,1:T(8,128)(2,1)S(1)}, bf16[192,1,128]{2,0,1:T(8,128)(2,1)S(1)}, u32[]{:S(2)}, u32[]{:S(2)}) collective-permute-start(bf16[192,1,128]{2,0,1:T(8,128)(2,1)S(1)} %copy.49), channel_id=1, source_target_pairs={{120,0},{0,8},{8,16},{16,24},{24,32},{32,40},{40,48},{48,56},{56,6... | collective-permute-start | bytes 147464 | tf_op jit(solution)/shard_map/while/body/eval_jaxpr/ppermute | solution.py:15
  484.0 13.4 %collective-permute-start.1 = (bf16[192,1,128]{2,0,1:T(8,128)(2,1)S(1)}, bf16[192,1,128]{2,0,1:T(8,128)(2,1)S(1)}, u32[]{:S(2)}, u32[]{:S(2)}) collective-permute-start(bf16[192,1,128]{2,0,1:T(8,128)(2,1)S(1)} %copy.50), channel_id=1, source_target_pairs={{120,0},{0,8},{8,16},{16,24},{24,32},{32,40},{40,48},{48,56},{56,6... | collective-permute-start | bytes 147464 | tf_op jit(solution)/shard_map/while/body/eval_jaxpr/ppermute | solution.py:15
  503.7 15.3 %collective-permute-start = (bf16[192,1,128]{2,0,1:T(8,128)(2,1)S(1)}, bf16[192,1,128]{2,0,1:T(8,128)(2,1)S(1)}, u32[]{:S(2)}, u32[]{:S(2)}) collective-permute-start(bf16[192,1,128]{2,0,1:T(8,128)(2,1)S(1)} %copy.49), channel_id=1, source_target_pairs={{120,0},{0,8},{8,16},{16,24},{24,32},{32,40},{40,48},{48,56},{56,6... | collective-permute-start | bytes 147464 | tf_op jit(solution)/shard_map/while/body/eval_jaxpr/ppermute | solution.py:15
  505.6 13.4 %collective-permute-start.1 = (bf16[192,1,128]{2,0,1:T(8,128)(2,1)S(1)}, bf16[192,1,128]{2,0,1:T(8,128)(2,1)S(1)}, u32[]{:S(2)}, u32[]{:S(2)}) collective-permute-start(bf16[192,1,128]{2,0,1:T(8,128)(2,1)S(1)} %copy.50), channel_id=1, source_target_pairs={{120,0},{0,8},{8,16},{16,24},{24,32},{32,40},{40,48},{48,56},{56,6... | collective-permute-start | bytes 147464 | tf_op jit(solution)/shard_map/while/body/eval_jaxpr/ppermute | solution.py:15
  525.3 15.3 %collective-permute-start = (bf16[192,1,128]{2,0,1:T(8,128)(2,1)S(1)}, bf16[192,1,128]{2,0,1:T(8,128)(2,1)S(1)}, u32[]{:S(2)}, u32[]{:S(2)}) collective-permute-start(bf16[192,1,128]{2,0,1:T(8,128)(2,1)S(1)} %copy.49), channel_id=1, source_target_pairs={{120,0},{0,8},{8,16},{16,24},{24,32},{32,40},{40,48},{48,56},{56,6... | collective-permute-start | bytes 147464 | tf_op jit(solution)/shard_map/while/body/eval_jaxpr/ppermute | solution.py:15
  546.9 15.3 %collective-permute-start = (bf16[192,1,128]{2,0,1:T(8,128)(2,1)S(1)}, bf16[192,1,128]{2,0,1:T(8,128)(2,1)S(1)}, u32[]{:S(2)}, u32[]{:S(2)}) collective-permute-start(bf16[192,1,128]{2,0,1:T(8,128)(2,1)S(1)} %copy.49), channel_id=1, source_target_pairs={{120,0},{0,8},{8,16},{16,24},{24,32},{32,40},{40,48},{48,56},{56,6... | collective-permute-start | bytes 147464 | tf_op jit(solution)/shard_map/while/body/eval_jaxpr/ppermute | solution.py:15
  (53 other events, 760.7 us)
Sparse Core Ops, SparseCore 0:
  10.2 129.0 all-gather.4
  577.0 439.2 reduce-scatter.3
